TPU v7x, 512 devices: a whole 4x8x8 slice. The times are simulated.
512 devices in a mesh: section: 4 (over z_lo, core), cls: 128 (over z_hi, x, y).
Axes of the slice: x: 4, y: 8, z: 8 (z_hi: 4, z_lo: 2; z = z_hi * 2 + z_lo), core: 2. Of those that a mesh axis runs over, the one named last changes fastest.
Arguments:
- images: bfloat16 [8192, 256, 256], P(('section', 'cls')), may hold values from -6 to 6
- group_ids: int32 [8192], P(('section', 'cls')), may hold values from 0 to 3
- row_filters: bfloat16 [4, 256, 256], replicated, may hold values from -0.375 to 0.375
- column_filters: bfloat16 [4, 256, 256], replicated, may hold values from -0.375 to 0.375
- basis_rows: bfloat16 [256, 16], replicated, may hold values from -0.375 to 0.375
- basis_columns: bfloat16 [256, 16], replicated, may hold values from -0.375 to 0.375
- rotations: bfloat16 [36, 256, 256], P('section'), may hold values from -0.375 to 0.375
- references: bfloat16 [256, 256], P('cls'), may hold values from -2 to 2
- sharpness: bfloat16 [8192], P(('section', 'cls')), may hold values from 0.049804688 to 2
- best_rotation: int32 [8192], P(('section', 'cls')), may hold values from 0 to 35
- assignments: int32 [8192, 32], P(('section', 'cls')), may hold values from 0 to 255, all different within a row; in each aligned block of 16 rows (0 to 15, 16 to 31, ...) at most 2 rows name the same one
Outputs:
- new_references: float32 [256, 256], P('cls')
- evidence: float32 [8192], P(('section', 'cls'))
Inputs may be any that keep to these rules, and one draw needn't show every extreme that they name: `assignments`: each particle lists 32 different classes; among the particles of one device no class is listed more than 2 times, a bound that some block reaches.
All inputs are finite; a program needn't handle non-finite values.
Results may differ from a plain program's by a relative error of at most 0.019.
Values may be sent and summed in bfloat16 or wider, within the bound.
A program may use at most 64 MiB of HBM per device.

v0:
```python
import math
import jax
import jax.numpy as jnp
from jax import lax
from jax.sharding import PartitionSpec as P

EPSILON = 1e-05


def soft_edge(pixels):
    coordinate = (jnp.arange(pixels, dtype=jnp.float32) - (pixels - 1) / 2.0) / (pixels / 2.0)
    radius = jnp.sqrt(
        coordinate[:, None] * coordinate[:, None] + coordinate[None, :] * coordinate[None, :]
    )
    falloff = jnp.clip((radius - 0.8) / 0.15, 0.0, 1.0)
    return 0.5 + 0.5 * jnp.cos(math.pi * falloff)


def filter_images(images, group_ids, row_filters, column_filters, basis_rows, basis_columns):
    column_each = jnp.take(column_filters, group_ids, axis=0)
    row_each = jnp.take(row_filters, group_ids, axis=0)
    filtered_half = jnp.einsum(
        "bij,bjk->bik", images, column_each, preferred_element_type=jnp.float32
    ).astype(jnp.bfloat16)
    filtered = jnp.einsum(
        "bij,bjk->bik", row_each, filtered_half, preferred_element_type=jnp.float32
    )
    masked = filtered * soft_edge(images.shape[1])
    power = jnp.mean(masked * masked, axis=(1, 2), keepdims=True)
    normed = (masked * lax.rsqrt(power + EPSILON)).astype(jnp.bfloat16)
    inner = jnp.einsum("bij,jk->bik", normed, basis_columns, preferred_element_type=jnp.float32)
    coeffs = jnp.einsum(
        "ja,bjk->bak", basis_rows.astype(jnp.float32), inner, precision=lax.Precision.HIGHEST
    )
    return coeffs.reshape(coeffs.shape[0], -1).astype(jnp.bfloat16)


def body(
    images,
    group_ids,
    row_filters,
    column_filters,
    basis_rows,
    basis_columns,
    rotations,
    references,
    sharpness,
    best_rotation,
    assignments,
):
    particles = images.shape[0]
    listed = assignments.shape[1]
    coeffs = filter_images(
        images, group_ids, row_filters, column_filters, basis_rows, basis_columns
    )
    gathered, gathered_sharp = (
        lax.all_gather(coeffs, "section", axis=0, tiled=True),
        lax.all_gather(sharpness, "section", axis=0, tiled=True),
    )
    gathered_best = lax.all_gather(best_rotation, "section", axis=0, tiled=True)
    all_refs = lax.all_gather(references, "cls", axis=0, tiled=True)
    classes = all_refs.shape[0]
    width = all_refs.shape[1]
    sections = lax.axis_size("section")
    local_rotations = rotations.shape[0]
    first_rotation = lax.axis_index("section") * local_rotations
    turned = jnp.einsum(
        "rkl,nl->nrk", rotations, gathered, preferred_element_type=jnp.float32
    ).astype(jnp.bfloat16)
    products = jnp.einsum("nrk,ck->nrc", turned, all_refs, preferred_element_type=jnp.float32)
    scores = products * gathered_sharp.astype(jnp.float32)[:, None, None]
    maxima = jnp.max(scores, axis=1)
    totals = jnp.sum(jnp.exp(scores - maxima[:, None, :]), axis=1)
    partial_marg = (maxima + jnp.log(totals)).reshape(sections, particles, classes)
    received_marg = lax.all_to_all(partial_marg, "section", split_axis=0, concat_axis=0, tiled=True)
    own_marg = jax.nn.logsumexp(received_marg, axis=0)
    evidence = jax.nn.logsumexp(own_marg, axis=1)
    class_range = jnp.arange(classes, dtype=jnp.int32)
    matches = assignments[:, :, None] == class_range[None, None, :]
    picked = jnp.sum(jnp.where(matches, own_marg[:, None, :], 0.0), axis=2)
    weights = jax.nn.softmax(picked, axis=1).astype(jnp.bfloat16)
    offset = gathered_best - first_rotation
    chosen = (offset[:, None] == jnp.arange(local_rotations, dtype=jnp.int32)[None, :]).astype(
        jnp.bfloat16
    )
    partial_rows = jnp.einsum("nrk,nr->nk", turned, chosen, preferred_element_type=jnp.float32)
    aligned = lax.psum_scatter(
        partial_rows.astype(jnp.bfloat16), "section", scatter_dimension=0, tiled=True
    )
    contribution = (
        weights.astype(jnp.float32)[:, :, None] * aligned.astype(jnp.float32)[:, None, :]
    ).astype(jnp.bfloat16)
    flat_classes = assignments.reshape(-1)
    flat_contribution = contribution.reshape(-1, width)
    flat_weights = weights.reshape(-1)
    owners = lax.axis_size("cls")
    own_classes = references.shape[0]
    capacity = max(2, -(-(particles * listed) // classes))
    onehot = (flat_classes[:, None] == class_range[None, :]).astype(jnp.int32)
    slot_rank = jnp.sum((jnp.cumsum(onehot, axis=0) - 1) * onehot, axis=1)
    slot_index = flat_classes * capacity + slot_rank
    buffer = (
        jnp.zeros((classes * capacity, width), jnp.bfloat16).at[slot_index].set(flat_contribution)
    )
    weight_slots = jnp.zeros((classes * capacity,), jnp.bfloat16).at[slot_index].set(flat_weights)
    buffer = buffer.reshape(owners, own_classes, capacity, width)
    weight_slots = weight_slots.reshape(owners, own_classes, capacity)
    received, received_weights = (
        lax.all_to_all(buffer, "cls", split_axis=0, concat_axis=0, tiled=True),
        lax.all_to_all(weight_slots, "cls", split_axis=0, concat_axis=0, tiled=True),
    )
    class_sums = jnp.sum(received.astype(jnp.float32), axis=(0, 2))
    class_weights = jnp.sum(received_weights.astype(jnp.float32), axis=(0, 2))
    class_sums, class_weights = lax.psum((class_sums, class_weights), "section")
    new_references = (class_sums + references.astype(jnp.float32)) / (class_weights[:, None] + 1.0)
    return (new_references, evidence)


def solution(mesh):
    in_specs = (
        P(("section", "cls"), None, None),
        P(("section", "cls")),
        P(),
        P(),
        P(),
        P(),
        P("section", None, None),
        P("cls", None),
        P(("section", "cls")),
        P(("section", "cls")),
        P(("section", "cls"), None),
    )
    out_specs = (P("cls", None), P(("section", "cls")))
    return jax.shard_map(body, mesh=mesh, in_specs=in_specs, out_specs=out_specs, check_vma=False)
```

profile of v0, /device:TPU:1, one launch (start us, length us, event | category | flops | bytes accessed | tf_op | source)
XLA Modules:
  0.0 496.1 jit_solution(2594808979812159641)
XLA Ops:
  7.2 0.8 compare_select_fusion.1
  8.7 3.1 gather_fusion
  11.8 2.0 gather_fusion.1
  13.8 1.0 multiply_add_fusion
  14.9 5.7 %multiply_reduce_fusion = (f32[16]{0:T(128)S(1)}, f32[16,256,256]{2,1,0:T(8,128)}) fusion(f32[256,256]{1,0:T(8,128)S(1)} %multiply_add_fusion, bf16[16,256,256]{2,1,0:T(8,128)(2,1)S(1)} %copy-done, bf16[16,256,256]{2,1,0:T(8,128)(2,1)} %gather_fusion.1, pred[16]{0:T(512)(128)(4,1)S(1)} %compare_and_fusion, bf16[16,256,256]{2,1,0:T(8,128)(2,1)} %gather_fusion), kind=kOutput, calls=%fused_computation.5 | convolution fusion | flops 1080033280 | bytes 10747984 | tf_op jit(solution)/shard_map/bij,bjk->bik/dot_general | solution.py:25
  20.6 3.0 fusion
  24.1 12.3 %all_gather.12 = bf16[64,256]{1,0:T(8,128)(2,1)} all-gather(bf16[16,256]{1,0:T(8,128)(2,1)S(1)} %convert_element_type.71), channel_id=1, replica_groups=mesh['section'=4,'cls'=128] {'section'}, dimensions={0}, use_global_device_ids=true | all-gather | bytes 40960 | tf_op jit(solution)/shard_map/all_gather | solution.py:57
  36.4 1.3 dynamic-slice
  38.6 5.2 %all-reduce = bf16[64]{0:T(256)(128)(2,1)S(1)} all-reduce(bf16[64]{0:T(256)(128)(2,1)S(1)} %dynamic-update-slice), channel_id=1, replica_groups=mesh['section'=4,'cls'=128] {'section'}, use_global_device_ids=true, to_apply=%add | all-reduce | flops 64 | bytes 256
  43.8 320.0 %all-gather = bf16[128,2,256]{2,1,0:T(2,128)(2,1)S(1)} all-gather(bf16[1,2,256]{2,1,0:T(2,128)(2,1)S(1)} %bitcast.40), channel_id=1, replica_groups=mesh['section'=4,'cls'=128] {'cls'}, dimensions={0}, use_global_device_ids=true | all-gather | bytes 132096 | tf_op jit(solution)/shard_map/all_gather | solution.py:61
  363.9 1.3 convolution_convert_fusion
  366.5 60.8 %all-to-all-start = ((f32[4,16,256]{2,1,0:T(8,128)}), f32[4,16,256]{2,1,0:T(8,128)S(1)}, u32[]{:S(2)}, u32[]{:S(2)}) async-start(f32[4,16,256]{2,1,0:T(8,128)} %bitcast.11), calls=%async_computation | async-start | bytes 131072 | tf_op jit(solution)/shard_map/all_to_all | solution.py:75
  427.6 4.2 all-reduce.1
  431.9 1.3 fusion.19
  435.8 3.8 scatter_custom_fusion.1
  439.6 0.8 reshape.197
  440.4 6.3 %all-to-all-start.2 = ((bf16[128,2,2]{2,1,0:T(2,128)(2,1)}), bf16[128,2,2]{2,1,0:T(2,128)(2,1)S(1)}, u32[]{:S(2)}, u32[]{:S(2)}) async-start(bf16[128,2,2]{2,1,0:T(2,128)(2,1)} %reshape.197), calls=%async_computation.3 | async-start | bytes 131072 | tf_op jit(solution)/shard_map/all_to_all | solution.py:110
  446.8 0.7 convert_element_type.78
  447.6 2.4 scatter_custom_fusion
  450.0 0.8 reshape.196
  450.8 8.5 %all-to-all-done.2 = bf16[128,2,2]{2,1,0:T(2,128)(2,1)S(1)} async-done(((bf16[128,2,2]{2,1,0:T(2,128)(2,1)}), bf16[128,2,2]{2,1,0:T(2,128)(2,1)S(1)}, u32[]{:S(2)}, u32[]{:S(2)}) %all-to-all-start.2) | async-done | bytes 1056 | tf_op jit(solution)/shard_map/all_to_all | solution.py:110
  459.3 7.2 %all-to-all-start.1 = ((bf16[128,2,2,256]{3,2,1,0:T(2,128)(2,1)}), bf16[128,2,2,256]{3,2,1,0:T(2,128)(2,1)S(1)}, u32[]{:S(2)}, u32[]{:S(2)}) async-start(bf16[128,2,2,256]{3,2,1,0:T(2,128)(2,1)} %reshape.196), calls=%async_computation.2 | async-start | bytes 524288 | tf_op jit(solution)/shard_map/all_to_all | solution.py:109
  467.5 12.7 %all-to-all-done.1 = bf16[128,2,2,256]{3,2,1,0:T(2,128)(2,1)S(1)} async-done(((bf16[128,2,2,256]{3,2,1,0:T(2,128)(2,1)}), bf16[128,2,2,256]{3,2,1,0:T(2,128)(2,1)S(1)}, u32[]{:S(2)}, u32[]{:S(2)}) %all-to-all-start.1) | async-done | bytes 262176 | tf_op jit(solution)/shard_map/all_to_all | solution.py:109
  480.3 8.3 %all-reduce.2 = (f32[2,256]{1,0:T(2,128)S(1)}, f32[2]{0:T(128)S(1)}) all-reduce(f32[2,256]{1,0:T(2,128)S(1)} %convert_reduce_fusion, f32[2]{0:T(128)S(1)} %convert_reduce_fusion.1), channel_id=1, replica_groups=mesh['section'=4,'cls'=128] {'section'}, use_global_device_ids=true, to_apply=%region_14.16 | all-reduce | flops 514 | bytes 4112 | tf_op jit(solution)/shard_map/psum | solution.py:114
  (74 shorter events, 7.6 us)
Async XLA Ops:
  7.2 7.7 %copy-start = (bf16[16,256,256]{2,1,0:T(8,128)(2,1)S(1)}, bf16[16,256,256]{2,1,0:T(8,128)(2,1)}, u32[]{:S(2)}) copy-start(bf16[16,256,256]{2,1,0:T(8,128)(2,1)} %param.13) | copy-start | bytes 6291460
  8.7 3.1 copy-start.1
  14.9 5.7 %copy-start.5 = (bf16[256,16]{0,1:T(8,128)(2,1)S(1)}, bf16[256,16]{0,1:T(8,128)(2,1)}, u32[]{:S(2)}) copy-start(bf16[256,16]{0,1:T(8,128)(2,1)} %param.18) | copy-start | bytes 24580
  20.6 3.1 copy-start.6
  20.6 17.8 %copy-start.8 = (bf16[16]{0:T(256)(128)(2,1)S(1)}, bf16[16]{0:T(256)(128)(2,1)}, u32[]{:S(2)}) copy-start(bf16[16]{0:T(256)(128)(2,1)} %param.21) | copy-start | bytes 100
  20.6 23.2 %copy-start.7 = (bf16[2,256]{1,0:T(2,128)(2,1)S(1)}, bf16[2,256]{1,0:T(2,128)(2,1)}, u32[]{:S(2)}) copy-start(bf16[2,256]{1,0:T(2,128)(2,1)} %param.20) | copy-start | bytes 3076
  20.6 343.3 %copy-start.2 = (bf16[9,256,256]{2,1,0:T(8,128)(2,1)S(1)}, bf16[9,256,256]{2,1,0:T(8,128)(2,1)}, u32[]{:S(2)}) copy-start(bf16[9,256,256]{2,1,0:T(8,128)(2,1)} %param.19) | copy-start | bytes 3538948
  24.0 403.3 %copy-start.9 = (s32[16]{0:T(128)S(1)}, s32[16]{0:T(128)}, u32[]{:S(2)}) copy-start(s32[16]{0:T(128)} %param.22) | copy-start | bytes 196
  363.8 70.0 %copy-start.4 = (s32[16,32]{1,0:T(8,128)S(1)}, s32[16,32]{1,0:T(8,128)}, u32[]{:S(2)}) copy-start(s32[16,32]{1,0:T(8,128)} %param.23) | copy-start | bytes 6148
  365.1 0.7 copy-start.3
  366.5 68.4 %all-to-all-start = ((f32[4,16,256]{2,1,0:T(8,128)}), f32[4,16,256]{2,1,0:T(8,128)S(1)}, u32[]{:S(2)}, u32[]{:S(2)}) async-start(f32[4,16,256]{2,1,0:T(8,128)} %bitcast.11), calls=%async_computation | async-start | bytes 131072 | tf_op jit(solution)/shard_map/all_to_all | solution.py:75
  427.3 19.4 %reduce-scatter.2.cloned.1.call-start = ((), (), s32[]{:S(2)}) async-start(), calls=%async_computation.4 | async-start | bytes 40960 | tf_op jit(solution)/shard_map/reduce_scatter | solution.py:87
  440.4 18.9 %all-to-all-start.2 = ((bf16[128,2,2]{2,1,0:T(2,128)(2,1)}), bf16[128,2,2]{2,1,0:T(2,128)(2,1)S(1)}, u32[]{:S(2)}, u32[]{:S(2)}) async-start(bf16[128,2,2]{2,1,0:T(2,128)(2,1)} %reshape.197), calls=%async_computation.3 | async-start | bytes 131072 | tf_op jit(solution)/shard_map/all_to_all | solution.py:110
  459.3 20.9 %all-to-all-start.1 = ((bf16[128,2,2,256]{3,2,1,0:T(2,128)(2,1)}), bf16[128,2,2,256]{3,2,1,0:T(2,128)(2,1)S(1)}, u32[]{:S(2)}, u32[]{:S(2)}) async-start(bf16[128,2,2,256]{3,2,1,0:T(2,128)(2,1)} %reshape.196), calls=%async_computation.2 | async-start | bytes 524288 | tf_op jit(solution)/shard_map/all_to_all | solution.py:109
Sparse Core Ops, SparseCore 0:
  433.9 11.9 reduce-scatter.1
where the time goes:
time: 497 us; the launch traced here: 496 us
  blocking collectives  350 us (70%)
  starting transfers between devices  74.3 us (15%)
  waiting for transfers between devices  21.3 us (4%)
  local copies, waits for them, and re-layouts  16.5 us (3%)
  between operations  15 us (3%)
  matrix products  11.8 us (2%)
  other arithmetic  7.26 us (1%)
    all_gather x1, blocking collectives, body(): all_refs = lax.all_gather(references, 'cls', axis=0, tiled=True)  320 us
    all_to_all x1, starting transfers between devices, body(): lax.all_to_all(partial_marg, 'section', split_axis=0, concat_axis=0, tile...  60.8 us
    all_to_all x1, waiting for transfers between devices, body(): lax.all_to_all(buffer, 'cls', split_axis=0, concat_axis=0, tiled=True)  12.7 us
    all_gather x1, blocking collectives, body(): lax.all_gather(coeffs, 'section', axis=0, tiled=True)  12.3 us
  transfers between devices with their start and end apart: 4, of which 2 were waited for; matrix products, arithmetic and copies ran while one was open for 3% of the time, Pallas kernels for 0%

commit v1 on v0

--- a/solution.py
+++ b/solution.py
@@ -54,7 +54,15 @@
         images, group_ids, row_filters, column_filters, basis_rows, basis_columns
     )
     gathered, gathered_sharp = (
-        lax.all_gather(coeffs, "section", axis=0, tiled=True),
+        jnp.concatenate(
+            lax.all_to_all(
+                jnp.stack([coeffs] * lax.axis_size("section"), axis=0),
+                axis_name="section",
+                split_axis=0,
+                concat_axis=0,
+            ),
+            0,
+        ),
         lax.all_gather(sharpness, "section", axis=0, tiled=True),
     )
     gathered_best = lax.all_gather(best_rotation, "section", axis=0, tiled=True)

time: 497 us -> 497 us (level)
  blocking collectives: 350 us -> 337 us
  starting transfers between devices: 74.3 us -> 84.6 us
    all_gather x1 -> x0, blocking collectives: 12.3 us -> none  [body(): lax.all_gather(coeffs, 'section', axis=0, tiled=True)]
    all_to_all x0 -> x1, starting transfers between devices: none -> 10.1 us  [body(): lax.all_to_all(jnp.stack([coeffs] * lax.axis_size('section'), axis=0), ax...]
  transfers between devices with their start and end apart: 4 -> 5, of which waited for: 2 -> 4; matrix products, arithmetic and copies ran while one was open for 3% -> 3% of each run, Pallas kernels for 0% -> 0%
where the time goes in v1:
time: 497 us
  blocking collectives  337 us (68%)
  starting transfers between devices  84.6 us (17%)
  waiting for transfers between devices  24.5 us (5%)
  local copies, waits for them, and re-layouts  16.7 us (3%)
  between operations  14.9 us (3%)
  matrix products  11.2 us (2%)
  other arithmetic  7.25 us (1%)
    all_gather x1, blocking collectives, body(): all_refs = lax.all_gather(references, 'cls', axis=0, tiled=True)  320 us
    all_to_all x1, starting transfers between devices, body(): lax.all_to_all(partial_marg, 'section', split_axis=0, concat_axis=0, tile...  60.6 us
    all_to_all x1, waiting for transfers between devices, body(): lax.all_to_all(buffer, 'cls', split_axis=0, concat_axis=0, tiled=True)  13.6 us
    all_to_all x1, starting transfers between devices, body(): lax.all_to_all(jnp.stack([coeffs] * lax.axis_size('section'), axis=0), ax...  10.1 us
  transfers between devices with their start and end apart: 5, of which 4 were waited for; matrix products, arithmetic and copies ran while one was open for 3% of the time, Pallas kernels for 0%

profile of v1, /device:TPU:1, one launch (start us, length us, event | category | flops | bytes accessed | tf_op | source)
XLA Modules:
  0.0 496.5 jit_solution(11070021180934977339)
XLA Ops:
  7.2 0.8 compare_select_fusion.1
  8.7 3.1 gather_fusion
  11.8 2.0 gather_fusion.1
  13.8 1.0 multiply_add_fusion
  14.9 5.7 %multiply_reduce_fusion = (f32[16]{0:T(128)S(1)}, f32[16,256,256]{2,1,0:T(8,128)}) fusion(f32[256,256]{1,0:T(8,128)S(1)} %multiply_add_fusion, bf16[16,256,256]{2,1,0:T(8,128)(2,1)S(1)} %copy-done, bf16[16,256,256]{2,1,0:T(8,128)(2,1)} %gather_fusion.1, pred[16]{0:T(512)(128)(4,1)S(1)} %compare_and_fusion, bf16[16,256,256]{2,1,0:T(8,128)(2,1)} %gather_fusion), kind=kOutput, calls=%fused_computation.5 | convolution fusion | flops 1080033280 | bytes 10747984 | tf_op jit(solution)/shard_map/bij,bjk->bik/dot_general | solution.py:25
  20.6 2.9 fusion
  24.6 10.1 %all-to-all-start = ((bf16[4,16,256]{2,1,0:T(8,128)(2,1)}), bf16[4,16,256]{2,1,0:T(8,128)(2,1)S(1)}, u32[]{:S(2)}, u32[]{:S(2)}) async-start(bf16[4,16,256]{2,1,0:T(8,128)(2,1)} %stack.2), calls=%async_computation | async-start | bytes 65536 | tf_op jit(solution)/shard_map/all_to_all | solution.py:58
  34.9 1.3 dynamic-slice
  37.1 5.4 %all-reduce = bf16[64]{0:T(256)(128)(2,1)S(1)} all-reduce(bf16[64]{0:T(256)(128)(2,1)S(1)} %dynamic-update-slice), channel_id=1, replica_groups=mesh['section'=4,'cls'=128] {'section'}, use_global_device_ids=true, to_apply=%add | all-reduce | flops 64 | bytes 256
  43.4 4.5 all-reduce.1
  48.2 320.0 %all-gather = bf16[128,2,256]{2,1,0:T(2,128)(2,1)S(1)} all-gather(bf16[1,2,256]{2,1,0:T(2,128)(2,1)S(1)} %bitcast.42), channel_id=1, replica_groups=mesh['section'=4,'cls'=128] {'cls'}, dimensions={0}, use_global_device_ids=true | all-gather | bytes 132096 | tf_op jit(solution)/shard_map/all_gather | solution.py:69
  368.3 1.8 convolution_convert_fusion
  371.1 60.6 %all-to-all-start.1 = ((f32[4,16,256]{2,1,0:T(8,128)}), f32[4,16,256]{2,1,0:T(8,128)S(1)}, u32[]{:S(2)}, u32[]{:S(2)}) async-start(f32[4,16,256]{2,1,0:T(8,128)} %bitcast.12), calls=%async_computation.1 | async-start | bytes 131072 | tf_op jit(solution)/shard_map/all_to_all | solution.py:83
  432.6 2.3 all-to-all-done.1
  435.8 3.8 scatter_custom_fusion.1
  439.6 0.8 reshape.204
  440.4 6.3 %all-to-all-start.3 = ((bf16[128,2,2]{2,1,0:T(2,128)(2,1)}), bf16[128,2,2]{2,1,0:T(2,128)(2,1)S(1)}, u32[]{:S(2)}, u32[]{:S(2)}) async-start(bf16[128,2,2]{2,1,0:T(2,128)(2,1)} %reshape.204), calls=%async_computation.4 | async-start | bytes 131072 | tf_op jit(solution)/shard_map/all_to_all | solution.py:118
  447.2 0.7 convert_element_type.80
  448.0 2.4 scatter_custom_fusion
  450.4 0.8 reshape.203
  451.2 8.1 %all-to-all-done.3 = bf16[128,2,2]{2,1,0:T(2,128)(2,1)S(1)} async-done(((bf16[128,2,2]{2,1,0:T(2,128)(2,1)}), bf16[128,2,2]{2,1,0:T(2,128)(2,1)S(1)}, u32[]{:S(2)}, u32[]{:S(2)}) %all-to-all-start.3) | async-done | bytes 1056 | tf_op jit(solution)/shard_map/all_to_all | solution.py:118
  459.3 7.6 %all-to-all-start.2 = ((bf16[128,2,2,256]{3,2,1,0:T(2,128)(2,1)}), bf16[128,2,2,256]{3,2,1,0:T(2,128)(2,1)S(1)}, u32[]{:S(2)}, u32[]{:S(2)}) async-start(bf16[128,2,2,256]{3,2,1,0:T(2,128)(2,1)} %reshape.203), calls=%async_computation.3 | async-start | bytes 524288 | tf_op jit(solution)/shard_map/all_to_all | solution.py:117
  467.9 13.6 %all-to-all-done.2 = bf16[128,2,2,256]{3,2,1,0:T(2,128)(2,1)S(1)} async-done(((bf16[128,2,2,256]{3,2,1,0:T(2,128)(2,1)}), bf16[128,2,2,256]{3,2,1,0:T(2,128)(2,1)S(1)}, u32[]{:S(2)}, u32[]{:S(2)}) %all-to-all-start.2) | async-done | bytes 262176 | tf_op jit(solution)/shard_map/all_to_all | solution.py:117
  481.6 7.4 %all-reduce.2 = (f32[2,256]{1,0:T(2,128)S(1)}, f32[2]{0:T(128)S(1)}) all-reduce(f32[2,256]{1,0:T(2,128)S(1)} %convert_reduce_fusion, f32[2]{0:T(128)S(1)} %convert_reduce_fusion.1), channel_id=1, replica_groups=mesh['section'=4,'cls'=128] {'section'}, use_global_device_ids=true, to_apply=%region_14.16 | all-reduce | flops 514 | bytes 4112 | tf_op jit(solution)/shard_map/psum | solution.py:122
  (72 shorter events, 8.6 us)
Async XLA Ops:
  7.2 7.7 %copy-start = (bf16[16,256,256]{2,1,0:T(8,128)(2,1)S(1)}, bf16[16,256,256]{2,1,0:T(8,128)(2,1)}, u32[]{:S(2)}) copy-start(bf16[16,256,256]{2,1,0:T(8,128)(2,1)} %param.13) | copy-start | bytes 6291460
  8.7 3.1 copy-start.1
  14.9 5.7 %copy-start.3 = (bf16[256,16]{0,1:T(8,128)(2,1)S(1)}, bf16[256,16]{0,1:T(8,128)(2,1)}, u32[]{:S(2)}) copy-start(bf16[256,16]{0,1:T(8,128)(2,1)} %param.18) | copy-start | bytes 24580
  20.6 3.0 copy-start.4
  20.6 14.2 %copy-start.2 = (s32[16,32]{1,0:T(8,128)S(1)}, s32[16,32]{1,0:T(8,128)}, u32[]{:S(2)}) copy-start(s32[16,32]{1,0:T(8,128)} %param.23) | copy-start | bytes 6148
  20.6 16.3 %copy-start.6 = (bf16[16]{0:T(256)(128)(2,1)S(1)}, bf16[16]{0:T(256)(128)(2,1)}, u32[]{:S(2)}) copy-start(bf16[16]{0:T(256)(128)(2,1)} %param.21) | copy-start | bytes 100
  23.5 19.7 %copy-start.7 = (s32[16]{0:T(128)S(1)}, s32[16]{0:T(128)}, u32[]{:S(2)}) copy-start(s32[16]{0:T(128)} %param.22) | copy-start | bytes 196
  23.5 24.7 %copy-start.5 = (bf16[2,256]{1,0:T(2,128)(2,1)S(1)}, bf16[2,256]{1,0:T(2,128)(2,1)}, u32[]{:S(2)}) copy-start(bf16[2,256]{1,0:T(2,128)(2,1)} %param.20) | copy-start | bytes 3076
  24.6 343.6 %all-to-all-start = ((bf16[4,16,256]{2,1,0:T(8,128)(2,1)}), bf16[4,16,256]{2,1,0:T(8,128)(2,1)S(1)}, u32[]{:S(2)}, u32[]{:S(2)}) async-start(bf16[4,16,256]{2,1,0:T(8,128)(2,1)} %stack.2), calls=%async_computation | async-start | bytes 65536 | tf_op jit(solution)/shard_map/all_to_all | solution.py:58
  371.1 63.8 %all-to-all-start.1 = ((f32[4,16,256]{2,1,0:T(8,128)}), f32[4,16,256]{2,1,0:T(8,128)S(1)}, u32[]{:S(2)}, u32[]{:S(2)}) async-start(f32[4,16,256]{2,1,0:T(8,128)} %bitcast.12), calls=%async_computation.1 | async-start | bytes 131072 | tf_op jit(solution)/shard_map/all_to_all | solution.py:83
  431.7 15.5 %reduce-scatter.2.cloned.1.call-start = ((), (), s32[]{:S(2)}) async-start(), calls=%async_computation.5 | async-start | bytes 40960 | tf_op jit(solution)/shard_map/reduce_scatter | solution.py:95
  440.4 18.9 %all-to-all-start.3 = ((bf16[128,2,2]{2,1,0:T(2,128)(2,1)}), bf16[128,2,2]{2,1,0:T(2,128)(2,1)S(1)}, u32[]{:S(2)}, u32[]{:S(2)}) async-start(bf16[128,2,2]{2,1,0:T(2,128)(2,1)} %reshape.204), calls=%async_computation.4 | async-start | bytes 131072 | tf_op jit(solution)/shard_map/all_to_all | solution.py:118
  459.3 22.2 %all-to-all-start.2 = ((bf16[128,2,2,256]{3,2,1,0:T(2,128)(2,1)}), bf16[128,2,2,256]{3,2,1,0:T(2,128)(2,1)S(1)}, u32[]{:S(2)}, u32[]{:S(2)}) async-start(bf16[128,2,2,256]{3,2,1,0:T(2,128)(2,1)} %reshape.203), calls=%async_computation.3 | async-start | bytes 524288 | tf_op jit(solution)/shard_map/all_to_all | solution.py:117
Sparse Core Ops, SparseCore 0:
  435.3 11.8 reduce-scatter.1
